TPU v7x, 256 devices: a whole 4x4x8 slice. The times are simulated.
256 devices in a mesh: layer: 8 (over y, core), feat: 32 (over z, x).
Axes of the slice: x: 4, y: 4, z: 8, core: 2. Of those that a mesh axis runs over, the one named last changes fastest.
Arguments:
- top_grad: bfloat16 [256, 4608], P('feat'), may hold values from -6 to 6
- decoder: bfloat16 [8, 16384, 4608], P('layer', 'feat'), may hold values from -0.09375 to 0.09375
- encoder: bfloat16 [8, 16384, 4608], P('layer', 'feat'), may hold values from -0.03125 to 0.03125
- activations: bfloat16 [8, 256, 16384], P('layer', None, 'feat'), may hold values from 0.099609375 to 3
- block_ids: int32 [8, 32, 64], P('layer'), may hold values from 0 to 127, all different within a row
- block_counts: int32 [8, 32], P('layer'), may hold values from 1 to 64, 1024 in all within a row
Outputs:
- attribution: bfloat16 [8, 256, 16384], P('layer', None, 'feat')
- grads: float32 [8, 256, 4608], P('layer', 'feat')
Inputs may be any that keep to these rules, and one draw needn't show every extreme that they name: `block_ids`: within one row of the last dimension the ids are distinct; every block id appears somewhere. `block_counts`: for each layer the counts sum to 1024, and some tile of each layer has exactly 64.
All inputs are finite; a program needn't handle non-finite values.
Results may differ from a plain program's by a relative error of at most 0.024.
Values may be sent and summed in bfloat16 or wider, within the bound.
A program may use at most 64 MiB of HBM per device.

v0:
```python
import jax
import jax.numpy as jnp
from jax import lax
from jax.sharding import PartitionSpec as P

BLOCK = 128


def passed_along(value, axis, steps):
    count = lax.axis_size(axis)
    first, last = (max(0, -steps), min(count, count - steps))
    return lax.ppermute(value, axis, [(source, source + steps) for source in range(first, last)])


def body(top_grad, decoder, encoder, activations, block_ids, block_counts):
    layer_count = lax.axis_size("layer")
    tile_count = lax.axis_size("feat")
    section_index = lax.axis_index("layer")
    feat_index = lax.axis_index("feat")
    dec_rows = decoder[0]
    enc_rows = encoder[0]
    feat_dev = dec_rows.shape[0]
    model_width = dec_rows.shape[1]
    blk_dev = feat_dev // BLOCK
    tok_dev = top_grad.shape[0]
    list_width = block_ids.shape[2]
    listed = jnp.arange(list_width, dtype=jnp.int32)[None, :] < block_counts[0][:, None]
    owned = feat_index * blk_dev + jnp.arange(blk_dev, dtype=jnp.int32)
    matches = (block_ids[0][:, :, None] == owned[None, None, :]) & listed[:, :, None]
    tile_mask = jnp.any(matches, axis=1).astype(jnp.bfloat16)
    gated = (
        activations[0].reshape(tile_count, tok_dev, blk_dev, BLOCK) * tile_mask[:, None, :, None]
    )
    gated = gated.reshape(tile_count, tok_dev, feat_dev)
    group_count = 4
    group_rows = tok_dev // group_count
    step_total = group_count + layer_count - 1
    is_top = section_index == layer_count - 1

    def advance(step_count, carry):
        incoming, attr_buf, grad_buf = carry
        group_index = step_count - (layer_count - 1 - section_index)
        is_live = (group_index >= 0) & (group_index < group_count)
        group_slot = jnp.clip(group_index, 0, group_count - 1)
        row_offset = group_slot * group_rows
        top_rows = lax.dynamic_slice_in_dim(top_grad, row_offset, group_rows, 0).astype(jnp.float32)
        upstream = jnp.where(is_top, top_rows, incoming)
        gate_rows = lax.dynamic_slice_in_dim(gated, row_offset, group_rows, 1).reshape(
            tile_count * group_rows, feat_dev
        )
        scores = lax.dot_general(
            lax.all_gather(upstream.astype(jnp.bfloat16), "feat", axis=0, tiled=True),
            dec_rows,
            (((1,), (1,)), ((), ())),
            preferred_element_type=jnp.float32,
        )
        attributed = (scores * gate_rows).astype(jnp.bfloat16)
        summed = lax.psum_scatter(
            jnp.dot(attributed, enc_rows, preferred_element_type=jnp.float32).astype(jnp.bfloat16),
            "feat",
            scatter_dimension=0,
            tiled=True,
        ).astype(jnp.float32)
        updated = upstream + summed
        old_attr = lax.dynamic_slice_in_dim(attr_buf, row_offset, group_rows, 1)
        new_attr = jnp.where(
            is_live, attributed.reshape(tile_count, group_rows, feat_dev), old_attr
        )
        attr_buf = lax.dynamic_update_slice_in_dim(attr_buf, new_attr, row_offset, 1)
        old_grad = lax.dynamic_slice_in_dim(grad_buf, row_offset, group_rows, 0)
        new_grad = jnp.where(is_live, updated, old_grad)
        grad_buf = lax.dynamic_update_slice_in_dim(grad_buf, new_grad, row_offset, 0)
        passed = passed_along(updated.astype(jnp.bfloat16), "layer", -1).astype(updated.dtype)
        return (passed, attr_buf, grad_buf)

    start_state = (
        jnp.zeros((group_rows, model_width), jnp.float32),
        jnp.zeros((tile_count, tok_dev, feat_dev), jnp.bfloat16),
        jnp.zeros((tok_dev, model_width), jnp.float32),
    )
    final_state = lax.fori_loop(0, step_total, advance, start_state)
    attr_out = final_state[1].reshape(1, tile_count * tok_dev, feat_dev)
    grad_out = final_state[2][None]
    return (attr_out, grad_out)


def solution(mesh):
    placed = (
        P("feat", None),
        P("layer", "feat", None),
        P("layer", "feat", None),
        P("layer", None, "feat"),
        P("layer", None, None),
        P("layer", None),
    )
    return jax.shard_map(
        body,
        mesh=mesh,
        in_specs=placed,
        out_specs=(P("layer", None, "feat"), P("layer", "feat", None)),
        check_vma=False,
    )
```

profile of v0, /device:TPU:1, one launch (start us, length us, event | category | flops | bytes accessed | tf_op | source)
XLA Modules:
  0.0 2294.9 jit_solution(4350635033827040506)
XLA Ops:
  10.1 2277.4 %while.20 = (s32[]{:T(128)}, f32[2,4608]{1,0:T(2,128)S(1)}, bf16[32,8,512]{2,1,0:T(8,128)(2,1)S(1)}, f32[8,4608]{1,0:T(8,128)S(1)}, pred[]{:T(512)}, /*index=5*/...) while((s32[]{:T(128)}, f32[2,4608]{1,0:T(2,128)S(1)}, ...), condition=%wide.region_3.4_spmd.clone, body=%wide.region_1.3_spmd.clone.sunk | while | flops 604802048 | bytes 36239852 | solution.py:81
  11.1 42.2 %all-gather.3 = bf16[32,2,4608]{2,1,0:T(2,128)(2,1)S(1)} all-gather(bf16[1,2,4608]{2,1,0:T(2,128)(2,1)S(1)} %convert_bitcast_fusion.2), channel_id=1, replica_groups=mesh['layer'=8,'feat'=32] {'feat'}, dimensions={0}, use_global_device_ids=true | all-gather | bytes 608256 | tf_op jit(solution)/shard_map/while/body/eval_jaxpr/all_gather | solution.py:52
  53.8 4.0 fusion.17
  57.8 1.8 convolution_convert_fusion.2
  60.8 152.3 %all-reduce.5.cloned.1.call-done = bf16[64,4608]{1,0:T(8,128)(2,1)} async-done(((bf16[64,4608]{1,0:T(8,128)(2,1)}), bf16[64,4608]{1,0:T(8,128)(2,1)}) %all-reduce.5.cloned.1.call-update) | async-done | bytes 589840 | tf_op jit(solution)/shard_map/while
  214.1 7.2 collective-permute-start
  221.4 2.4 collective-permute-done
  224.8 36.7 %all-gather.3 = bf16[32,2,4608]{2,1,0:T(2,128)(2,1)S(1)} all-gather(bf16[1,2,4608]{2,1,0:T(2,128)(2,1)S(1)} %convert_bitcast_fusion.2), channel_id=1, replica_groups=mesh['layer'=8,'feat'=32] {'feat'}, dimensions={0}, use_global_device_ids=true | all-gather | bytes 608256 | tf_op jit(solution)/shard_map/while/body/eval_jaxpr/all_gather | solution.py:52
  261.9 4.0 fusion.17
  269.0 150.5 %all-reduce.5.cloned.1.call-done = bf16[64,4608]{1,0:T(8,128)(2,1)} async-done(((bf16[64,4608]{1,0:T(8,128)(2,1)}), bf16[64,4608]{1,0:T(8,128)(2,1)}) %all-reduce.5.cloned.1.call-update) | async-done | bytes 589840 | tf_op jit(solution)/shard_map/while
  420.5 7.2 collective-permute-start
  427.8 2.4 collective-permute-done
  431.2 36.7 %all-gather.3 = bf16[32,2,4608]{2,1,0:T(2,128)(2,1)S(1)} all-gather(bf16[1,2,4608]{2,1,0:T(2,128)(2,1)S(1)} %convert_bitcast_fusion.2), channel_id=1, replica_groups=mesh['layer'=8,'feat'=32] {'feat'}, dimensions={0}, use_global_device_ids=true | all-gather | bytes 608256 | tf_op jit(solution)/shard_map/while/body/eval_jaxpr/all_gather | solution.py:52
  468.3 4.0 fusion.17
  472.3 1.8 convolution_convert_fusion.2
  475.4 150.5 %all-reduce.5.cloned.1.call-done = bf16[64,4608]{1,0:T(8,128)(2,1)} async-done(((bf16[64,4608]{1,0:T(8,128)(2,1)}), bf16[64,4608]{1,0:T(8,128)(2,1)}) %all-reduce.5.cloned.1.call-update) | async-done | bytes 589840 | tf_op jit(solution)/shard_map/while
  626.8 7.2 collective-permute-start
  634.2 2.4 collective-permute-done
  637.6 36.7 %all-gather.3 = bf16[32,2,4608]{2,1,0:T(2,128)(2,1)S(1)} all-gather(bf16[1,2,4608]{2,1,0:T(2,128)(2,1)S(1)} %convert_bitcast_fusion.2), channel_id=1, replica_groups=mesh['layer'=8,'feat'=32] {'feat'}, dimensions={0}, use_global_device_ids=true | all-gather | bytes 608256 | tf_op jit(solution)/shard_map/while/body/eval_jaxpr/all_gather | solution.py:52
  674.7 4.0 fusion.17
  678.7 1.8 convolution_convert_fusion.2
  681.8 150.5 %all-reduce.5.cloned.1.call-done = bf16[64,4608]{1,0:T(8,128)(2,1)} async-done(((bf16[64,4608]{1,0:T(8,128)(2,1)}), bf16[64,4608]{1,0:T(8,128)(2,1)}) %all-reduce.5.cloned.1.call-update) | async-done | bytes 589840 | tf_op jit(solution)/shard_map/while
  833.2 7.2 collective-permute-start
  840.6 2.4 collective-permute-done
  843.9 36.7 %all-gather.3 = bf16[32,2,4608]{2,1,0:T(2,128)(2,1)S(1)} all-gather(bf16[1,2,4608]{2,1,0:T(2,128)(2,1)S(1)} %convert_bitcast_fusion.2), channel_id=1, replica_groups=mesh['layer'=8,'feat'=32] {'feat'}, dimensions={0}, use_global_device_ids=true | all-gather | bytes 608256 | tf_op jit(solution)/shard_map/while/body/eval_jaxpr/all_gather | solution.py:52
  881.1 4.0 fusion.17
  885.1 1.8 convolution_convert_fusion.2
  888.1 150.5 %all-reduce.5.cloned.1.call-done = bf16[64,4608]{1,0:T(8,128)(2,1)} async-done(((bf16[64,4608]{1,0:T(8,128)(2,1)}), bf16[64,4608]{1,0:T(8,128)(2,1)}) %all-reduce.5.cloned.1.call-update) | async-done | bytes 589840 | tf_op jit(solution)/shard_map/while
  1039.6 7.2 collective-permute-start
  1046.9 2.4 collective-permute-done
  1050.3 36.7 %all-gather.3 = bf16[32,2,4608]{2,1,0:T(2,128)(2,1)S(1)} all-gather(bf16[1,2,4608]{2,1,0:T(2,128)(2,1)S(1)} %convert_bitcast_fusion.2), channel_id=1, replica_groups=mesh['layer'=8,'feat'=32] {'feat'}, dimensions={0}, use_global_device_ids=true | all-gather | bytes 608256 | tf_op jit(solution)/shard_map/while/body/eval_jaxpr/all_gather | solution.py:52
  1087.4 4.0 fusion.17
  1091.5 1.8 convolution_convert_fusion.2
  1094.5 150.5 %all-reduce.5.cloned.1.call-done = bf16[64,4608]{1,0:T(8,128)(2,1)} async-done(((bf16[64,4608]{1,0:T(8,128)(2,1)}), bf16[64,4608]{1,0:T(8,128)(2,1)}) %all-reduce.5.cloned.1.call-update) | async-done | bytes 589840 | tf_op jit(solution)/shard_map/while
  1246.0 7.2 collective-permute-start
  1253.3 2.4 collective-permute-done
  1256.7 36.7 %all-gather.3 = bf16[32,2,4608]{2,1,0:T(2,128)(2,1)S(1)} all-gather(bf16[1,2,4608]{2,1,0:T(2,128)(2,1)S(1)} %convert_bitcast_fusion.2), channel_id=1, replica_groups=mesh['layer'=8,'feat'=32] {'feat'}, dimensions={0}, use_global_device_ids=true | all-gather | bytes 608256 | tf_op jit(solution)/shard_map/while/body/eval_jaxpr/all_gather | solution.py:52
  1293.8 4.0 fusion.17
  1297.8 1.8 convolution_convert_fusion.2
  1300.9 150.5 %all-reduce.5.cloned.1.call-done = bf16[64,4608]{1,0:T(8,128)(2,1)} async-done(((bf16[64,4608]{1,0:T(8,128)(2,1)}), bf16[64,4608]{1,0:T(8,128)(2,1)}) %all-reduce.5.cloned.1.call-update) | async-done | bytes 589840 | tf_op jit(solution)/shard_map/while
  1452.3 7.2 collective-permute-start
  1459.7 2.4 collective-permute-done
  1463.1 36.7 %all-gather.3 = bf16[32,2,4608]{2,1,0:T(2,128)(2,1)S(1)} all-gather(bf16[1,2,4608]{2,1,0:T(2,128)(2,1)S(1)} %convert_bitcast_fusion.2), channel_id=1, replica_groups=mesh['layer'=8,'feat'=32] {'feat'}, dimensions={0}, use_global_device_ids=true | all-gather | bytes 608256 | tf_op jit(solution)/shard_map/while/body/eval_jaxpr/all_gather | solution.py:52
  1500.2 4.0 fusion.17
  1507.3 150.5 %all-reduce.5.cloned.1.call-done = bf16[64,4608]{1,0:T(8,128)(2,1)} async-done(((bf16[64,4608]{1,0:T(8,128)(2,1)}), bf16[64,4608]{1,0:T(8,128)(2,1)}) %all-reduce.5.cloned.1.call-update) | async-done | bytes 589840 | tf_op jit(solution)/shard_map/while
  1658.7 7.2 collective-permute-start
  1666.1 2.4 collective-permute-done
  1669.4 36.7 %all-gather.3 = bf16[32,2,4608]{2,1,0:T(2,128)(2,1)S(1)} all-gather(bf16[1,2,4608]{2,1,0:T(2,128)(2,1)S(1)} %convert_bitcast_fusion.2), channel_id=1, replica_groups=mesh['layer'=8,'feat'=32] {'feat'}, dimensions={0}, use_global_device_ids=true | all-gather | bytes 608256 | tf_op jit(solution)/shard_map/while/body/eval_jaxpr/all_gather | solution.py:52
  1706.6 4.0 fusion.17
  1713.6 150.5 %all-reduce.5.cloned.1.call-done = bf16[64,4608]{1,0:T(8,128)(2,1)} async-done(((bf16[64,4608]{1,0:T(8,128)(2,1)}), bf16[64,4608]{1,0:T(8,128)(2,1)}) %all-reduce.5.cloned.1.call-update) | async-done | bytes 589840 | tf_op jit(solution)/shard_map/while
  1865.1 7.2 collective-permute-start
  1872.4 2.4 collective-permute-done
  1875.8 36.7 %all-gather.3 = bf16[32,2,4608]{2,1,0:T(2,128)(2,1)S(1)} all-gather(bf16[1,2,4608]{2,1,0:T(2,128)(2,1)S(1)} %convert_bitcast_fusion.2), channel_id=1, replica_groups=mesh['layer'=8,'feat'=32] {'feat'}, dimensions={0}, use_global_device_ids=true | all-gather | bytes 608256 | tf_op jit(solution)/shard_map/while/body/eval_jaxpr/all_gather | solution.py:52
  1912.9 4.0 fusion.17
  1917.0 1.8 convolution_convert_fusion.2
  1920.0 150.5 %all-reduce.5.cloned.1.call-done = bf16[64,4608]{1,0:T(8,128)(2,1)} async-done(((bf16[64,4608]{1,0:T(8,128)(2,1)}), bf16[64,4608]{1,0:T(8,128)(2,1)}) %all-reduce.5.cloned.1.call-update) | async-done | bytes 589840 | tf_op jit(solution)/shard_map/while
  2071.5 7.2 collective-permute-start
  2078.8 2.4 collective-permute-done
  2082.2 36.7 %all-gather.3 = bf16[32,2,4608]{2,1,0:T(2,128)(2,1)S(1)} all-gather(bf16[1,2,4608]{2,1,0:T(2,128)(2,1)S(1)} %convert_bitcast_fusion.2), channel_id=1, replica_groups=mesh['layer'=8,'feat'=32] {'feat'}, dimensions={0}, use_global_device_ids=true | all-gather | bytes 608256 | tf_op jit(solution)/shard_map/while/body/eval_jaxpr/all_gather | solution.py:52
  2119.3 4.0 fusion.17
  2123.3 1.8 convolution_convert_fusion.2
  2126.4 150.5 %all-reduce.5.cloned.1.call-done = bf16[64,4608]{1,0:T(8,128)(2,1)} async-done(((bf16[64,4608]{1,0:T(8,128)(2,1)}), bf16[64,4608]{1,0:T(8,128)(2,1)}) %all-reduce.5.cloned.1.call-update) | async-done | bytes 589840 | tf_op jit(solution)/shard_map/while
  2277.8 7.2 collective-permute-start
  2285.2 2.4 collective-permute-done
  (183 shorter events, 43.7 us)
Async XLA Ops:
  10.2 202.9 %all-reduce.5.cloned.1.call-start = ((), (), s32[]{:S(2)}) async-start(), calls=%async_computation | async-start | bytes 1179648 | tf_op jit(solution)/shard_map/while
  53.7 4.0 copy-start
  53.7 5.9 copy-start.3
  214.1 9.7 collective-permute-start
  223.8 195.6 %all-reduce.5.cloned.1.call-start = ((), (), s32[]{:S(2)}) async-start(), calls=%async_computation | async-start | bytes 1179648 | tf_op jit(solution)/shard_map/while
  261.9 4.0 copy-start
  261.9 5.9 copy-start.3
  420.5 9.7 collective-permute-start
  430.2 195.6 %all-reduce.5.cloned.1.call-start = ((), (), s32[]{:S(2)}) async-start(), calls=%async_computation | async-start | bytes 1179648 | tf_op jit(solution)/shard_map/while
  468.3 4.0 copy-start
  468.3 5.9 copy-start.3
  626.8 9.7 collective-permute-start
  636.6 195.6 %all-reduce.5.cloned.1.call-start = ((), (), s32[]{:S(2)}) async-start(), calls=%async_computation | async-start | bytes 1179648 | tf_op jit(solution)/shard_map/while
  674.7 4.0 copy-start
  674.7 5.9 copy-start.3
  833.2 9.7 collective-permute-start
  843.0 195.6 %all-reduce.5.cloned.1.call-start = ((), (), s32[]{:S(2)}) async-start(), calls=%async_computation | async-start | bytes 1179648 | tf_op jit(solution)/shard_map/while
  881.0 4.0 copy-start
  881.1 5.9 copy-start.3
  1039.6 9.7 collective-permute-start
  1049.3 195.6 %all-reduce.5.cloned.1.call-start = ((), (), s32[]{:S(2)}) async-start(), calls=%async_computation | async-start | bytes 1179648 | tf_op jit(solution)/shard_map/while
  1087.4 4.0 copy-start
  1087.4 5.9 copy-start.3
  1246.0 9.7 collective-permute-start
  1255.7 195.6 %all-reduce.5.cloned.1.call-start = ((), (), s32[]{:S(2)}) async-start(), calls=%async_computation | async-start | bytes 1179648 | tf_op jit(solution)/shard_map/while
  1293.8 4.0 copy-start
  1293.8 5.9 copy-start.3
  1452.3 9.7 collective-permute-start
  1462.1 195.6 %all-reduce.5.cloned.1.call-start = ((), (), s32[]{:S(2)}) async-start(), calls=%async_computation | async-start | bytes 1179648 | tf_op jit(solution)/shard_map/while
  1500.2 4.0 copy-start
  1500.2 5.9 copy-start.3
  1658.7 9.7 collective-permute-start
  1668.5 195.6 %all-reduce.5.cloned.1.call-start = ((), (), s32[]{:S(2)}) async-start(), calls=%async_computation | async-start | bytes 1179648 | tf_op jit(solution)/shard_map/while
  1706.5 4.0 copy-start
  1706.6 5.9 copy-start.3
  1865.1 9.7 collective-permute-start
  1874.8 195.6 %all-reduce.5.cloned.1.call-start = ((), (), s32[]{:S(2)}) async-start(), calls=%async_computation | async-start | bytes 1179648 | tf_op jit(solution)/shard_map/while
  1912.9 4.0 copy-start
  1912.9 5.9 copy-start.3
  2071.5 9.7 collective-permute-start
  2081.2 195.6 %all-reduce.5.cloned.1.call-start = ((), (), s32[]{:S(2)}) async-start(), calls=%async_computation | async-start | bytes 1179648 | tf_op jit(solution)/shard_map/while
  2119.3 4.0 copy-start
  2119.3 5.9 copy-start.3
  2277.8 9.7 collective-permute-start
  2287.6 0.7 copy-start.1
  2287.6 0.7 copy-start.2
Sparse Core Ops, SparseCore 0:
  59.7 153.3 all-reduce.4
  267.9 151.5 all-reduce.4
  474.3 151.5 all-reduce.4
  680.6 151.5 all-reduce.4
  887.0 151.5 all-reduce.4
  1093.4 151.5 all-reduce.4
  1299.8 151.5 all-reduce.4
  1506.1 151.5 all-reduce.4
  1712.5 151.5 all-reduce.4
  1918.9 151.5 all-reduce.4
  2125.3 151.5 all-reduce.4
where the time goes:
time: 2300 us; the launch traced here: 2290 us
  waiting for transfers between devices  1680 us (73%)
  blocking collectives  409 us (18%)
  starting transfers between devices  79.4 us (3%)
  matrix products  63.8 us (3%)
  other arithmetic  26.4 us (1%)
    while x22, waiting for transfers between devices  1660 us
    all_gather x11, blocking collectives, advance(): lax.all_gather(upstream.astype(jnp.bfloat16), 'feat', axis=0, tiled=True)  409 us
    ppermute x11, starting transfers between devices, passed_along(): lax.ppermute(value, axis, [(source, source + steps) for source in range(f...  78.9 us
  transfers between devices with their start and end apart: 22, of which 22 were waited for; matrix products, arithmetic and copies ran while one was open for 0% of the time, Pallas kernels for 0%

commit v1 on v0

--- a/solution.py
+++ b/solution.py
@@ -2,8 +2,15 @@
 import jax.numpy as jnp
 from jax import lax
 from jax.sharding import PartitionSpec as P
+from jax.lax import all_to_all, axis_size
 
 BLOCK = 128
+
+
+def manage_the_floor(own_rows, axis_name):
+    return jnp.concatenate(
+        all_to_all(jnp.stack([own_rows] * axis_size(axis_name), 0), axis_name, 0, 0), axis=0
+    )
 
 
 def passed_along(value, axis, steps):
@@ -49,7 +56,7 @@
             tile_count * group_rows, feat_dev
         )
         scores = lax.dot_general(
-            lax.all_gather(upstream.astype(jnp.bfloat16), "feat", axis=0, tiled=True),
+            manage_the_floor(upstream.astype(jnp.bfloat16), "feat"),
             dec_rows,
             (((1,), (1,)), ((), ())),
             preferred_element_type=jnp.float32,

time: 2300 us -> 2050 us (0.89)
  blocking collectives: 409 us -> 0 us
  waiting for transfers between devices: 1680 us -> 1760 us
  starting transfers between devices: 79.4 us -> 148 us
    all_gather x11 -> x0, blocking collectives: 409 us -> none  [advance(): lax.all_gather(upstream.astype(jnp.bfloat16), 'feat', axis=0, tiled=True)]
    all_to_all x0 -> x11, waiting for transfers between devices: none -> 200 us  [manage_the_floor(): all_to_all(jnp.stack([own_rows] * axis_size(axis_name), 0), axis_name, 0, 0)]
    while x22, waiting for transfers between devices: 1660 us -> 1530 us
    all_to_all x0 -> x11, starting transfers between devices: none -> 68.2 us  [manage_the_floor(): all_to_all(jnp.stack([own_rows] * axis_size(axis_name), 0), axis_name, 0, 0)]
  transfers between devices with their start and end apart: 22 -> 33, of which waited for: 22 -> 33; matrix products, arithmetic and copies ran while one was open for 0% -> 1% of each run, Pallas kernels for 0% -> 0%
where the time goes in v1:
time: 2050 us
  waiting for transfers between devices  1760 us (86%)
  starting transfers between devices  148 us (7%)
  matrix products  63.7 us (3%)
  other arithmetic  26.4 us (1%)
  local copies, waits for them, and re-layouts  24.1 us (1%)
    while x22, waiting for transfers between devices  1530 us
    all_to_all x11, waiting for transfers between devices, manage_the_floor(): all_to_all(jnp.stack([own_rows] * axis_size(axis_name), 0), axis_name, 0, 0)  200 us
    ppermute x11, starting transfers between devices, passed_along(): lax.ppermute(value, axis, [(source, source + steps) for source in range(f...  78.9 us
    all_to_all x11, starting transfers between devices, manage_the_floor(): all_to_all(jnp.stack([own_rows] * axis_size(axis_name), 0), axis_name, 0, 0)  68.2 us
    dot_general x11, matrix products, advance(): lax.dot_general(manage_the_floor(upstream.astype(jnp.bfloat16), 'feat'),...  44.2 us
  transfers between devices with their start and end apart: 33, of which 33 were waited for; matrix products, arithmetic and copies ran while one was open for 1% of the time, Pallas kernels for 0%

profile of v1, /device:TPU:1, one launch (start us, length us, event | category | flops | bytes accessed | tf_op | source)
XLA Modules:
  0.0 2045.4 jit_solution(17402794585922310879)
XLA Ops:
  10.1 2027.9 %while.20 = (s32[]{:T(128)}, f32[2,4608]{1,0:T(2,128)S(1)}, bf16[32,8,512]{2,1,0:T(8,128)(2,1)S(1)}, f32[8,4608]{1,0:T(8,128)S(1)}, pred[]{:T(512)}, /*index=5*/...) while((s32[]{:T(128)}, f32[2,4608]{1,0:T(2,128)S(1)}, ...), condition=%wide.region_3.4_spmd.clone, body=%wide.region_1.3_spmd.clone.sunk | while | flops 604802048 | bytes 38009356 | solution.py:88
  12.2 11.9 all-to-all-start
  24.3 17.4 all-to-all-done
  41.9 4.0 fusion.20
  49.0 141.3 %all-reduce.5.cloned.1.call-done = bf16[64,4608]{1,0:T(8,128)(2,1)} async-done(((bf16[64,4608]{1,0:T(8,128)(2,1)}), bf16[64,4608]{1,0:T(8,128)(2,1)}) %all-reduce.5.cloned.1.call-update) | async-done | bytes 589840 | tf_op jit(solution)/shard_map/while
  191.3 7.2 collective-permute-start
  198.6 2.4 collective-permute-done
  203.1 5.6 all-to-all-start
  209.0 18.3 all-to-all-done
  227.5 4.0 fusion.20
  234.7 139.3 %all-reduce.5.cloned.1.call-done = bf16[64,4608]{1,0:T(8,128)(2,1)} async-done(((bf16[64,4608]{1,0:T(8,128)(2,1)}), bf16[64,4608]{1,0:T(8,128)(2,1)}) %all-reduce.5.cloned.1.call-update) | async-done | bytes 589840 | tf_op jit(solution)/shard_map/while
  375.0 7.2 collective-permute-start
  382.3 2.4 collective-permute-done
  386.8 5.6 all-to-all-start
  392.7 18.3 all-to-all-done
  411.2 4.0 fusion.20
  418.3 139.3 %all-reduce.5.cloned.1.call-done = bf16[64,4608]{1,0:T(8,128)(2,1)} async-done(((bf16[64,4608]{1,0:T(8,128)(2,1)}), bf16[64,4608]{1,0:T(8,128)(2,1)}) %all-reduce.5.cloned.1.call-update) | async-done | bytes 589840 | tf_op jit(solution)/shard_map/while
  558.7 7.2 collective-permute-start
  566.0 2.4 collective-permute-done
  570.5 5.6 all-to-all-start
  576.4 18.3 all-to-all-done
  594.9 4.0 fusion.20
  602.0 139.4 %all-reduce.5.cloned.1.call-done = bf16[64,4608]{1,0:T(8,128)(2,1)} async-done(((bf16[64,4608]{1,0:T(8,128)(2,1)}), bf16[64,4608]{1,0:T(8,128)(2,1)}) %all-reduce.5.cloned.1.call-update) | async-done | bytes 589840 | tf_op jit(solution)/shard_map/while
  742.4 7.2 collective-permute-start
  749.8 2.4 collective-permute-done
  754.2 5.6 all-to-all-start
  760.1 18.3 all-to-all-done
  778.6 4.0 fusion.20
  785.8 139.3 %all-reduce.5.cloned.1.call-done = bf16[64,4608]{1,0:T(8,128)(2,1)} async-done(((bf16[64,4608]{1,0:T(8,128)(2,1)}), bf16[64,4608]{1,0:T(8,128)(2,1)}) %all-reduce.5.cloned.1.call-update) | async-done | bytes 589840 | tf_op jit(solution)/shard_map/while
  926.1 7.2 collective-permute-start
  933.5 2.4 collective-permute-done
  937.9 5.6 all-to-all-start
  943.8 18.3 all-to-all-done
  962.3 4.0 fusion.20
  969.5 139.3 %all-reduce.5.cloned.1.call-done = bf16[64,4608]{1,0:T(8,128)(2,1)} async-done(((bf16[64,4608]{1,0:T(8,128)(2,1)}), bf16[64,4608]{1,0:T(8,128)(2,1)}) %all-reduce.5.cloned.1.call-update) | async-done | bytes 589840 | tf_op jit(solution)/shard_map/while
  1109.8 7.2 collective-permute-start
  1117.2 2.4 collective-permute-done
  1121.6 5.6 all-to-all-start
  1127.5 18.3 all-to-all-done
  1146.0 4.0 fusion.20
  1153.2 139.4 %all-reduce.5.cloned.1.call-done = bf16[64,4608]{1,0:T(8,128)(2,1)} async-done(((bf16[64,4608]{1,0:T(8,128)(2,1)}), bf16[64,4608]{1,0:T(8,128)(2,1)}) %all-reduce.5.cloned.1.call-update) | async-done | bytes 589840 | tf_op jit(solution)/shard_map/while
  1293.5 7.2 collective-permute-start
  1300.9 2.4 collective-permute-done
  1305.3 5.6 all-to-all-start
  1311.2 18.3 all-to-all-done
  1329.7 4.0 fusion.20
  1336.9 139.3 %all-reduce.5.cloned.1.call-done = bf16[64,4608]{1,0:T(8,128)(2,1)} async-done(((bf16[64,4608]{1,0:T(8,128)(2,1)}), bf16[64,4608]{1,0:T(8,128)(2,1)}) %all-reduce.5.cloned.1.call-update) | async-done | bytes 589840 | tf_op jit(solution)/shard_map/while
  1477.2 7.2 collective-permute-start
  1489.0 5.6 all-to-all-start
  1494.9 18.3 all-to-all-done
  1513.4 4.0 fusion.20
  1520.6 139.3 %all-reduce.5.cloned.1.call-done = bf16[64,4608]{1,0:T(8,128)(2,1)} async-done(((bf16[64,4608]{1,0:T(8,128)(2,1)}), bf16[64,4608]{1,0:T(8,128)(2,1)}) %all-reduce.5.cloned.1.call-update) | async-done | bytes 589840 | tf_op jit(solution)/shard_map/while
  1660.9 7.2 collective-permute-start
  1668.3 2.4 collective-permute-done
  1672.7 5.6 all-to-all-start
  1678.6 18.3 all-to-all-done
  1697.1 4.0 fusion.20
  1704.3 139.4 %all-reduce.5.cloned.1.call-done = bf16[64,4608]{1,0:T(8,128)(2,1)} async-done(((bf16[64,4608]{1,0:T(8,128)(2,1)}), bf16[64,4608]{1,0:T(8,128)(2,1)}) %all-reduce.5.cloned.1.call-update) | async-done | bytes 589840 | tf_op jit(solution)/shard_map/while
  1844.7 7.2 collective-permute-start
  1856.5 5.6 all-to-all-start
  1862.3 18.3 all-to-all-done
  1880.9 4.0 fusion.20
  1888.0 139.3 %all-reduce.5.cloned.1.call-done = bf16[64,4608]{1,0:T(8,128)(2,1)} async-done(((bf16[64,4608]{1,0:T(8,128)(2,1)}), bf16[64,4608]{1,0:T(8,128)(2,1)}) %all-reduce.5.cloned.1.call-update) | async-done | bytes 589840 | tf_op jit(solution)/shard_map/while
  2028.3 7.2 collective-permute-start
  (205 shorter events, 77.8 us)
Async XLA Ops:
  12.2 29.4 %all-to-all-start = ((bf16[32,2,4608]{2,1,0:T(2,128)(2,1)}), bf16[32,2,4608]{2,1,0:T(2,128)(2,1)S(1)}, u32[]{:S(2)}, u32[]{:S(2)}) async-start(bf16[32,2,4608]{2,1,0:T(2,128)(2,1)} %stack.8), calls=%async_computation | async-start | bytes 1179648 | tf_op jit(solution)/shard_map/while/body/eval_jaxpr/all_to_all | solution.py:12
  24.1 166.2 %all-reduce.5.cloned.1.call-start = ((), (), s32[]{:S(2)}) async-start(), calls=%async_computation.1 | async-start | bytes 1179648 | tf_op jit(solution)/shard_map/while
  41.9 4.1 copy-start
  41.9 5.9 copy-start.3
  191.3 9.7 collective-permute-start
  203.1 24.1 %all-to-all-start = ((bf16[32,2,4608]{2,1,0:T(2,128)(2,1)}), bf16[32,2,4608]{2,1,0:T(2,128)(2,1)S(1)}, u32[]{:S(2)}, u32[]{:S(2)}) async-start(bf16[32,2,4608]{2,1,0:T(2,128)(2,1)} %stack.8), calls=%async_computation | async-start | bytes 1179648 | tf_op jit(solution)/shard_map/while/body/eval_jaxpr/all_to_all | solution.py:12
  208.8 165.2 %all-reduce.5.cloned.1.call-start = ((), (), s32[]{:S(2)}) async-start(), calls=%async_computation.1 | async-start | bytes 1179648 | tf_op jit(solution)/shard_map/while
  227.5 4.1 copy-start
  227.5 5.9 copy-start.3
  375.0 9.7 collective-permute-start
  386.8 24.1 %all-to-all-start = ((bf16[32,2,4608]{2,1,0:T(2,128)(2,1)}), bf16[32,2,4608]{2,1,0:T(2,128)(2,1)S(1)}, u32[]{:S(2)}, u32[]{:S(2)}) async-start(bf16[32,2,4608]{2,1,0:T(2,128)(2,1)} %stack.8), calls=%async_computation | async-start | bytes 1179648 | tf_op jit(solution)/shard_map/while/body/eval_jaxpr/all_to_all | solution.py:12
  392.4 165.2 %all-reduce.5.cloned.1.call-start = ((), (), s32[]{:S(2)}) async-start(), calls=%async_computation.1 | async-start | bytes 1179648 | tf_op jit(solution)/shard_map/while
  411.2 4.0 copy-start
  411.2 5.9 copy-start.3
  558.7 9.7 collective-permute-start
  570.5 24.1 %all-to-all-start = ((bf16[32,2,4608]{2,1,0:T(2,128)(2,1)}), bf16[32,2,4608]{2,1,0:T(2,128)(2,1)S(1)}, u32[]{:S(2)}, u32[]{:S(2)}) async-start(bf16[32,2,4608]{2,1,0:T(2,128)(2,1)} %stack.8), calls=%async_computation | async-start | bytes 1179648 | tf_op jit(solution)/shard_map/while/body/eval_jaxpr/all_to_all | solution.py:12
  576.1 165.3 %all-reduce.5.cloned.1.call-start = ((), (), s32[]{:S(2)}) async-start(), calls=%async_computation.1 | async-start | bytes 1179648 | tf_op jit(solution)/shard_map/while
  594.9 4.0 copy-start
  594.9 5.9 copy-start.3
  742.4 9.7 collective-permute-start
  754.2 24.1 %all-to-all-start = ((bf16[32,2,4608]{2,1,0:T(2,128)(2,1)}), bf16[32,2,4608]{2,1,0:T(2,128)(2,1)S(1)}, u32[]{:S(2)}, u32[]{:S(2)}) async-start(bf16[32,2,4608]{2,1,0:T(2,128)(2,1)} %stack.8), calls=%async_computation | async-start | bytes 1179648 | tf_op jit(solution)/shard_map/while/body/eval_jaxpr/all_to_all | solution.py:12
  759.9 165.2 %all-reduce.5.cloned.1.call-start = ((), (), s32[]{:S(2)}) async-start(), calls=%async_computation.1 | async-start | bytes 1179648 | tf_op jit(solution)/shard_map/while
  778.6 4.0 copy-start
  778.6 5.9 copy-start.3
  926.1 9.7 collective-permute-start
  937.9 24.1 %all-to-all-start = ((bf16[32,2,4608]{2,1,0:T(2,128)(2,1)}), bf16[32,2,4608]{2,1,0:T(2,128)(2,1)S(1)}, u32[]{:S(2)}, u32[]{:S(2)}) async-start(bf16[32,2,4608]{2,1,0:T(2,128)(2,1)} %stack.8), calls=%async_computation | async-start | bytes 1179648 | tf_op jit(solution)/shard_map/while/body/eval_jaxpr/all_to_all | solution.py:12
  943.6 165.2 %all-reduce.5.cloned.1.call-start = ((), (), s32[]{:S(2)}) async-start(), calls=%async_computation.1 | async-start | bytes 1179648 | tf_op jit(solution)/shard_map/while
  962.3 4.0 copy-start
  962.3 5.9 copy-start.3
  1109.8 9.7 collective-permute-start
  1121.6 24.1 %all-to-all-start = ((bf16[32,2,4608]{2,1,0:T(2,128)(2,1)}), bf16[32,2,4608]{2,1,0:T(2,128)(2,1)S(1)}, u32[]{:S(2)}, u32[]{:S(2)}) async-start(bf16[32,2,4608]{2,1,0:T(2,128)(2,1)} %stack.8), calls=%async_computation | async-start | bytes 1179648 | tf_op jit(solution)/shard_map/while/body/eval_jaxpr/all_to_all | solution.py:12
  1127.3 165.3 %all-reduce.5.cloned.1.call-start = ((), (), s32[]{:S(2)}) async-start(), calls=%async_computation.1 | async-start | bytes 1179648 | tf_op jit(solution)/shard_map/while
  1146.0 4.0 copy-start
  1146.0 5.9 copy-start.3
  1293.5 9.7 collective-permute-start
  1305.3 24.1 %all-to-all-start = ((bf16[32,2,4608]{2,1,0:T(2,128)(2,1)}), bf16[32,2,4608]{2,1,0:T(2,128)(2,1)S(1)}, u32[]{:S(2)}, u32[]{:S(2)}) async-start(bf16[32,2,4608]{2,1,0:T(2,128)(2,1)} %stack.8), calls=%async_computation | async-start | bytes 1179648 | tf_op jit(solution)/shard_map/while/body/eval_jaxpr/all_to_all | solution.py:12
  1311.0 165.2 %all-reduce.5.cloned.1.call-start = ((), (), s32[]{:S(2)}) async-start(), calls=%async_computation.1 | async-start | bytes 1179648 | tf_op jit(solution)/shard_map/while
  1329.7 4.0 copy-start
  1329.7 5.9 copy-start.3
  1477.2 9.7 collective-permute-start
  1489.0 24.1 %all-to-all-start = ((bf16[32,2,4608]{2,1,0:T(2,128)(2,1)}), bf16[32,2,4608]{2,1,0:T(2,128)(2,1)S(1)}, u32[]{:S(2)}, u32[]{:S(2)}) async-start(bf16[32,2,4608]{2,1,0:T(2,128)(2,1)} %stack.8), calls=%async_computation | async-start | bytes 1179648 | tf_op jit(solution)/shard_map/while/body/eval_jaxpr/all_to_all | solution.py:12
  1494.7 165.2 %all-reduce.5.cloned.1.call-start = ((), (), s32[]{:S(2)}) async-start(), calls=%async_computation.1 | async-start | bytes 1179648 | tf_op jit(solution)/shard_map/while
  1513.4 4.0 copy-start
  1513.4 5.9 copy-start.3
  1660.9 9.7 collective-permute-start
  1672.7 24.1 %all-to-all-start = ((bf16[32,2,4608]{2,1,0:T(2,128)(2,1)}), bf16[32,2,4608]{2,1,0:T(2,128)(2,1)S(1)}, u32[]{:S(2)}, u32[]{:S(2)}) async-start(bf16[32,2,4608]{2,1,0:T(2,128)(2,1)} %stack.8), calls=%async_computation | async-start | bytes 1179648 | tf_op jit(solution)/shard_map/while/body/eval_jaxpr/all_to_all | solution.py:12
  1678.4 165.3 %all-reduce.5.cloned.1.call-start = ((), (), s32[]{:S(2)}) async-start(), calls=%async_computation.1 | async-start | bytes 1179648 | tf_op jit(solution)/shard_map/while
  1697.1 4.0 copy-start
  1697.1 5.9 copy-start.3
  1844.7 9.7 collective-permute-start
  1856.5 24.1 %all-to-all-start = ((bf16[32,2,4608]{2,1,0:T(2,128)(2,1)}), bf16[32,2,4608]{2,1,0:T(2,128)(2,1)S(1)}, u32[]{:S(2)}, u32[]{:S(2)}) async-start(bf16[32,2,4608]{2,1,0:T(2,128)(2,1)} %stack.8), calls=%async_computation | async-start | bytes 1179648 | tf_op jit(solution)/shard_map/while/body/eval_jaxpr/all_to_all | solution.py:12
  1862.1 165.2 %all-reduce.5.cloned.1.call-start = ((), (), s32[]{:S(2)}) async-start(), calls=%async_computation.1 | async-start | bytes 1179648 | tf_op jit(solution)/shard_map/while
  1880.8 4.0 copy-start
  1880.8 5.9 copy-start.3
  2028.3 9.7 collective-permute-start
  2038.1 0.7 copy-start.1
  2038.1 0.7 copy-start.2
Sparse Core Ops, SparseCore 0:
  47.9 142.3 all-reduce.4
  233.5 140.4 all-reduce.4
  417.2 140.4 all-reduce.4
  600.9 140.5 all-reduce.4
  784.6 140.4 all-reduce.4
  968.3 140.4 all-reduce.4
  1152.0 140.5 all-reduce.4
  1335.7 140.4 all-reduce.4
  1519.4 140.4 all-reduce.4
  1703.1 140.5 all-reduce.4
  1886.8 140.4 all-reduce.4
